TPU v7x, 32 devices: a whole 2x2x4 slice. The times are simulated.
32 devices in a mesh: seq: 8 (over y, x, core), dp: 4 (over z).
Axes of the slice: x: 2, y: 2, z: 4, core: 2. Of those that a mesh axis runs over, the one named last changes fastest.
Arguments:
- tokens: bfloat16 [4, 4096, 1024], P('dp', 'seq'), may hold values from -6 to 6
- item_starts: int32 [4, 8], P('dp', 'seq'), may hold values from 0 to 1, as said below
- attn_gain: float32 [1024], replicated, may hold values from 0.5 to 1.5
- query_weight: bfloat16 [1024, 1024], replicated, may hold values from -0.1875 to 0.1875
- key_weight: bfloat16 [1024, 1024], replicated, may hold values from -0.1875 to 0.1875
- value_weight: bfloat16 [1024, 1024], replicated, may hold values from -0.1875 to 0.1875
- output_weight: bfloat16 [1024, 1024], replicated, may hold values from -1.5 to 1.5
- state_queries: bfloat16 [512, 1024], replicated, may hold values from -6 to 6
- state_weight: bfloat16 [1024, 2048], replicated, may hold values from -1.5 to 1.5
- gate_bias: float32 [1024], replicated, may hold values from -2 to 6
- initial_state: float32 [512, 1024], replicated, may hold values from -6 to 6
- mlp_gain: float32 [1024], replicated, may hold values from 0.5 to 1.5
- up_weight: bfloat16 [1024, 4096], replicated, may hold values from -0.1875 to 0.1875
- down_weight: bfloat16 [4096, 1024], replicated, may hold values from -0.09375 to 0.09375
- out_cotangent: bfloat16 [4, 4096, 1024], P('dp', 'seq'), may hold values from -6 to 6
- state_cotangent: float32 [4, 8, 512, 1024], P('dp', 'seq'), may hold values from -6 to 6
Outputs:
- mixed: bfloat16 [4, 4096, 1024], P('dp', 'seq')
- states: float32 [4, 8, 512, 1024], P('dp', 'seq')
- tokens_grad: float32 [4, 4096, 1024], P('dp', 'seq')
- attn_gain_grad: float32 [1024], P('seq')
- query_grad: float32 [1024, 1024], P('seq')
- key_grad: float32 [1024, 1024], P('seq')
- value_grad: float32 [1024, 1024], P('seq')
- output_grad: float32 [1024, 1024], P('seq')
- state_queries_grad: float32 [512, 1024], P('seq')
- state_weight_grad: float32 [1024, 2048], P('seq')
- gate_bias_grad: float32 [1024], P('seq')
- initial_state_grad: float32 [512, 1024], P('seq')
- mlp_gain_grad: float32 [1024], P('seq')
- up_grad: float32 [1024, 4096], P('seq')
- down_grad: float32 [4096, 1024], P('seq')
Inputs may be any that keep to these rules, and one draw needn't show every extreme that they name: item_starts is 1 exactly at the first block of each item. Block 0 of every group starts an item; each aligned run of 8 blocks holds one item of 8 blocks or two of 4 blocks; some item has 8 blocks.
All inputs are finite; a program needn't handle non-finite values.
Results may differ from a plain program's by a relative error of at most 0.023.
Values may be sent and summed in bfloat16 or wider, within the bound.
No kernel may reach another device: no remote copies, remote signals or barrier semaphores. Data moves between devices by JAX's collectives and lax.ppermute only.
A program may use at most 512 MiB of HBM per device.

v0:
```python
import math
import jax
import jax.numpy as jnp
from jax import lax
from jax.sharding import PartitionSpec as P

D = 1024
HEADS = 8
HEAD_DIM = 128
W = 512
NS = 512
EPSILON = 1e-06
NEGATIVE = -1e30
GELU_SCALE = 0.7978845608028654
GELU_CUBIC = 0.044715


def shifted(value, axis, steps):
    count = lax.axis_size(axis)
    first, last = (max(0, -steps), min(count, count - steps))
    return lax.ppermute(value, axis, [(source, source + steps) for source in range(first, last)])


def entering(value, axis, join, neutral):
    count, mine = (lax.axis_size(axis), lax.axis_index(axis))
    pieces = jax.tree.map(lambda part: lax.all_gather(part, axis), value)
    so_far = jax.tree.map(
        lambda part, zero: jnp.full_like(part, 0) + jnp.asarray(zero, part.dtype), value, neutral
    )

    def lap(position, so_far):
        longer = join(so_far, jax.tree.map(lambda part: part[position], pieces))
        return jax.tree.map(lambda new, old: jnp.where(position < mine, new, old), longer, so_far)

    return lax.fori_loop(0, count - 1, lap, so_far)


def carried_in(x, axis, join, neutral):
    count = lax.axis_size(axis)
    place = lax.axis_index(axis)
    ahead = count - 1 - place
    gathered = jax.tree.map(
        lambda a, kind: lax.all_gather(a.astype(kind), axis), x, (jnp.bfloat16, jnp.bfloat16)
    )
    state = jax.tree.map(lambda a, e: jnp.zeros_like(a) + jnp.asarray(e, a.dtype), x, neutral)

    def one(lap, state):
        source = count - 1 - lap
        return join(
            state,
            jax.tree.map(
                lambda a, own: lax.dynamic_index_in_dim(a, source, 0, False).astype(own.dtype),
                gathered,
                x,
            ),
        )

    return lax.fori_loop(0, ahead, one, state)


def gelu_tanh(upper):
    inner = GELU_SCALE * (upper + GELU_CUBIC * upper * upper * upper)
    return 0.5 * upper * (1.0 + jnp.tanh(inner))


def gelu_slope(upper):
    inner = GELU_SCALE * (upper + GELU_CUBIC * upper * upper * upper)
    tvalue = jnp.tanh(inner)
    return 0.5 * (1.0 + tvalue) + 0.5 * upper * (1.0 - tvalue * tvalue) * GELU_SCALE * (
        1.0 + 3.0 * GELU_CUBIC * upper * upper
    )


def product(left, right):
    return jnp.dot(left, right, preferred_element_type=jnp.float32)


def product_tn(left, right):
    return lax.dot_general(
        left, right, (((0,), (0,)), ((), ())), preferred_element_type=jnp.float32
    )


def product_nt(left, right):
    return lax.dot_general(
        left, right, (((1,), (1,)), ((), ())), preferred_element_type=jnp.float32
    )


def rms_scale(field):
    return lax.rsqrt(jnp.mean(field * field, axis=-1, keepdims=True) + EPSILON)


def rms_back(field, scaled, gain, grad):
    gain_grad = jnp.sum(grad * field * scaled, axis=0)
    weighted = grad * gain
    field_grad = scaled * weighted - field * scaled * scaled * scaled * jnp.mean(
        weighted * field, axis=-1, keepdims=True
    )
    return (gain_grad, field_grad)


def split_heads(field):
    return field.reshape(field.shape[0], HEADS, HEAD_DIM)


def compose(earlier, later):
    return (later[0] * earlier[0], later[0] * earlier[1] + later[1])


def key_mask(keep_left):
    rows = lax.broadcasted_iota(jnp.int32, (W, 2 * W + NS), 0)
    cols = lax.broadcasted_iota(jnp.int32, (W, 2 * W + NS), 1)
    left_part = (cols < W) & keep_left
    own_part = (cols >= W) & (cols < 2 * W) & (cols - W <= rows)
    return left_part | own_part | (cols >= 2 * W)


def body(
    tokens,
    item_starts,
    attn_gain,
    query_weight,
    key_weight,
    value_weight,
    output_weight,
    state_queries,
    state_weight,
    gate_bias,
    initial_state,
    mlp_gain,
    up_weight,
    down_weight,
    out_cotangent,
    state_cotangent,
):
    scale = 1.0 / math.sqrt(HEAD_DIM)
    inputs = tokens[0].astype(jnp.float32)
    start_flag = item_starts[0, 0]
    start = start_flag.astype(jnp.float32)
    keep = 1.0 - start
    attn_scale = rms_scale(inputs)
    normed = (inputs * attn_scale * attn_gain).astype(jnp.bfloat16)
    queries = product(normed, query_weight).astype(jnp.bfloat16)
    keys = product(normed, key_weight).astype(jnp.bfloat16)
    values = product(normed, value_weight).astype(jnp.bfloat16)
    left_pair = shifted(jnp.stack([keys, values]), "seq", 1)
    left_keys = left_pair[0]
    left_values = left_pair[1]
    query_heads = split_heads(state_queries)
    key_heads = split_heads(keys)
    value_heads = split_heads(values)
    summary_raw = (
        jnp.einsum("nhd,whd->hnw", query_heads, key_heads, preferred_element_type=jnp.float32)
        * scale
    )
    summary_peak = jnp.max(summary_raw, axis=-1, keepdims=True)
    summary_exp = jnp.exp(summary_raw - summary_peak)
    summary_total = jnp.sum(summary_exp, axis=-1, keepdims=True)
    summary_lse = summary_peak + jnp.log(summary_total)
    summary_low = (summary_exp / summary_total).astype(jnp.bfloat16)
    summary = jnp.einsum(
        "hnw,whd->nhd", summary_low, value_heads, preferred_element_type=jnp.float32
    )
    summary = summary.reshape(NS, D).astype(jnp.bfloat16)
    projected = product(summary, state_weight)
    update = projected[:, :D]
    forget = jax.nn.sigmoid(projected[:, D:] + gate_bias)
    fresh = (1.0 - forget) * update
    carried_scale = keep * forget
    carried_base = start * forget * initial_state + fresh
    identity = (jnp.ones((NS, D), jnp.float32), jnp.zeros((NS, D), jnp.float32))
    prefix = entering((carried_scale, carried_base), "seq", compose, identity)
    previous = prefix[1]
    state_in = keep * previous + start * initial_state
    state_out = forget * state_in + fresh
    state_low = state_in.astype(jnp.bfloat16)
    state_keys = product(state_low, key_weight).astype(jnp.bfloat16)
    state_values = product(state_low, value_weight).astype(jnp.bfloat16)
    seen_keys = split_heads(jnp.concatenate([left_keys, keys, state_keys], axis=0))
    seen_values = split_heads(jnp.concatenate([left_values, values, state_values], axis=0))
    token_heads = split_heads(queries)
    valid = key_mask(start_flag == 0)
    raw = jnp.einsum("whd,khd->hwk", token_heads, seen_keys, preferred_element_type=jnp.float32)
    scores = jnp.where(valid, raw * scale, NEGATIVE)
    peak = jnp.max(scores, axis=-1, keepdims=True)
    expos = jnp.exp(scores - peak)
    totals = jnp.sum(expos, axis=-1, keepdims=True)
    log_total = peak + jnp.log(totals)
    probs_low = (expos / totals).astype(jnp.bfloat16)
    attended = jnp.einsum(
        "hwk,khd->whd", probs_low, seen_values, preferred_element_type=jnp.float32
    )
    attended = attended.reshape(W, D).astype(jnp.bfloat16)
    hidden = inputs + product(attended, output_weight)
    mlp_scale = rms_scale(hidden)
    normed_mlp = (hidden * mlp_scale * mlp_gain).astype(jnp.bfloat16)
    upper = product(normed_mlp, up_weight)
    activated = gelu_tanh(upper).astype(jnp.bfloat16)
    mixed = (hidden + product(activated, down_weight)).astype(jnp.bfloat16)
    cotangent = out_cotangent[0]
    down_grad = product_tn(activated, cotangent)
    activated_grad = product_nt(cotangent, down_weight).astype(jnp.bfloat16)
    upper_grad = (activated_grad.astype(jnp.float32) * gelu_slope(upper)).astype(jnp.bfloat16)
    up_grad = product_tn(normed_mlp, upper_grad)
    normed_mlp_grad = product_nt(upper_grad, up_weight)
    mlp_gain_grad, hidden_part = rms_back(hidden, mlp_scale, mlp_gain, normed_mlp_grad)
    hidden_grad = hidden_part + cotangent.astype(jnp.float32)
    attended_grad = hidden_grad.astype(jnp.bfloat16)
    output_grad = product_tn(attended, attended_grad)
    attended_heads_grad = split_heads(product_nt(attended_grad, output_weight).astype(jnp.bfloat16))
    again = jnp.einsum("whd,khd->hwk", token_heads, seen_keys, preferred_element_type=jnp.float32)
    probs = jnp.exp(jnp.where(valid, again * scale, NEGATIVE) - log_total)
    probs_again = probs.astype(jnp.bfloat16)
    prob_grad = jnp.einsum(
        "whd,khd->hwk", attended_heads_grad, seen_values, preferred_element_type=jnp.float32
    )
    seen_values_grad = jnp.einsum(
        "hwk,whd->khd", probs_again, attended_heads_grad, preferred_element_type=jnp.float32
    ).reshape(2 * W + NS, D)
    rowdot = jnp.sum(probs * prob_grad, axis=-1, keepdims=True)
    score_grad = (probs * (prob_grad - rowdot) * scale).astype(jnp.bfloat16)
    queries_grad = (
        jnp.einsum("hwk,khd->whd", score_grad, seen_keys, preferred_element_type=jnp.float32)
        .reshape(W, D)
        .astype(jnp.bfloat16)
    )
    seen_keys_grad = jnp.einsum(
        "hwk,whd->khd", score_grad, token_heads, preferred_element_type=jnp.float32
    ).reshape(2 * W + NS, D)
    state_keys_grad = seen_keys_grad[2 * W :].astype(jnp.bfloat16)
    state_values_grad = seen_values_grad[2 * W :].astype(jnp.bfloat16)
    direct = product_nt(state_keys_grad, key_weight) + product_nt(state_values_grad, value_weight)
    state_cot = state_cotangent[0, 0]
    back_scale = keep * forget
    back_base = keep * (forget * state_cot + direct)
    suffix = carried_in((back_scale, back_base), "seq", compose, identity)
    incoming = suffix[1]
    out_state_grad = state_cot + incoming
    in_state_grad = forget * out_state_grad + direct
    initial_state_grad = start * in_state_grad
    gate_grad = out_state_grad * (state_in - update) * forget * (1.0 - forget)
    gate_bias_grad = jnp.sum(gate_grad, axis=0)
    projected_grad = jnp.concatenate([out_state_grad * (1.0 - forget), gate_grad], axis=1).astype(
        jnp.bfloat16
    )
    state_weight_grad = product_tn(summary, projected_grad)
    summary_grad = split_heads(product_nt(projected_grad, state_weight).astype(jnp.bfloat16))
    summary_again = jnp.einsum(
        "nhd,whd->hnw", query_heads, key_heads, preferred_element_type=jnp.float32
    )
    summary_probs = jnp.exp(summary_again * scale - summary_lse)
    summary_prob_grad = jnp.einsum(
        "nhd,whd->hnw", summary_grad, value_heads, preferred_element_type=jnp.float32
    )
    summary_rowdot = jnp.sum(summary_probs * summary_prob_grad, axis=-1, keepdims=True)
    summary_score_grad = (summary_probs * (summary_prob_grad - summary_rowdot) * scale).astype(
        jnp.bfloat16
    )
    state_queries_grad = jnp.einsum(
        "hnw,whd->nhd", summary_score_grad, key_heads, preferred_element_type=jnp.float32
    ).reshape(NS, D)
    keys_from_summary = jnp.einsum(
        "hnw,nhd->whd", summary_score_grad, query_heads, preferred_element_type=jnp.float32
    ).reshape(W, D)
    values_from_summary = jnp.einsum(
        "hnw,nhd->whd", summary_low, summary_grad, preferred_element_type=jnp.float32
    ).reshape(W, D)
    returned = shifted(
        jnp.stack([seen_keys_grad[:W], seen_values_grad[:W]]).astype(jnp.bfloat16), "seq", -1
    ).astype(jnp.float32)
    keys_total = (seen_keys_grad[W : 2 * W] + keys_from_summary + returned[0]).astype(jnp.bfloat16)
    values_total = (seen_values_grad[W : 2 * W] + values_from_summary + returned[1]).astype(
        jnp.bfloat16
    )
    query_grad = product_tn(normed, queries_grad)
    key_grad = product_tn(normed, keys_total) + product_tn(state_low, state_keys_grad)
    value_grad = product_tn(normed, values_total) + product_tn(state_low, state_values_grad)
    normed_grad = (
        product_nt(queries_grad, query_weight)
        + product_nt(keys_total, key_weight)
        + product_nt(values_total, value_weight)
    )
    attn_gain_grad, token_part = rms_back(inputs, attn_scale, attn_gain, normed_grad)
    tokens_grad = hidden_grad + token_part
    whole = (
        lax.psum_scatter(
            attn_gain_grad.astype(jnp.bfloat16), "seq", scatter_dimension=0, tiled=True
        ).astype(jnp.float32),
        lax.psum_scatter(
            query_grad.astype(jnp.bfloat16), "seq", scatter_dimension=0, tiled=True
        ).astype(jnp.float32),
        lax.psum_scatter(
            key_grad.astype(jnp.bfloat16), "seq", scatter_dimension=0, tiled=True
        ).astype(jnp.float32),
        lax.psum_scatter(
            value_grad.astype(jnp.bfloat16), "seq", scatter_dimension=0, tiled=True
        ).astype(jnp.float32),
        lax.psum_scatter(
            output_grad.astype(jnp.bfloat16), "seq", scatter_dimension=0, tiled=True
        ).astype(jnp.float32),
        lax.psum_scatter(
            state_queries_grad.astype(jnp.bfloat16), "seq", scatter_dimension=0, tiled=True
        ).astype(jnp.float32),
        lax.psum_scatter(
            state_weight_grad.astype(jnp.bfloat16), "seq", scatter_dimension=0, tiled=True
        ).astype(jnp.float32),
        lax.psum_scatter(
            gate_bias_grad.astype(jnp.bfloat16), "seq", scatter_dimension=0, tiled=True
        ).astype(jnp.float32),
        lax.psum_scatter(
            initial_state_grad.astype(jnp.bfloat16), "seq", scatter_dimension=0, tiled=True
        ).astype(jnp.float32),
        lax.psum_scatter(
            mlp_gain_grad.astype(jnp.bfloat16), "seq", scatter_dimension=0, tiled=True
        ).astype(jnp.float32),
        lax.psum_scatter(
            up_grad.astype(jnp.bfloat16), "seq", scatter_dimension=0, tiled=True
        ).astype(jnp.float32),
        lax.psum_scatter(
            down_grad.astype(jnp.bfloat16), "seq", scatter_dimension=0, tiled=True
        ).astype(jnp.float32),
    )
    summed = tuple(
        (
            lax.psum(whole[0].astype(jnp.bfloat16), "dp").astype(jnp.float32),
            lax.psum(whole[1].astype(jnp.bfloat16), "dp").astype(jnp.float32),
            lax.psum(whole[2].astype(jnp.bfloat16), "dp").astype(jnp.float32),
            lax.psum(whole[3].astype(jnp.bfloat16), "dp").astype(jnp.float32),
            lax.psum(whole[4].astype(jnp.bfloat16), "dp").astype(jnp.float32),
            lax.psum(whole[5].astype(jnp.bfloat16), "dp").astype(jnp.float32),
            lax.psum(whole[6].astype(jnp.bfloat16), "dp").astype(jnp.float32),
            lax.psum(whole[7].astype(jnp.bfloat16), "dp").astype(jnp.float32),
            lax.psum(whole[8].astype(jnp.bfloat16), "dp").astype(jnp.float32),
            lax.psum(whole[9].astype(jnp.bfloat16), "dp").astype(jnp.float32),
            lax.psum(whole[10].astype(jnp.bfloat16), "dp").astype(jnp.float32),
            lax.psum(whole[11].astype(jnp.bfloat16), "dp").astype(jnp.float32),
        )
    )
    return (
        mixed[None],
        state_out[None, None],
        tokens_grad[None],
        summed[0],
        summed[1],
        summed[2],
        summed[3],
        summed[4],
        summed[5],
        summed[6],
        summed[7],
        summed[8],
        summed[9],
        summed[10],
        summed[11],
    )


def solution(mesh):
    in_specs = (
        P("dp", "seq", None),
        P("dp", "seq"),
        P(),
        P(),
        P(),
        P(),
        P(),
        P(),
        P(),
        P(),
        P(),
        P(),
        P(),
        P(),
        P("dp", "seq", None),
        P("dp", "seq", None, None),
    )
    out_specs = (
        P("dp", "seq", None),
        P("dp", "seq", None, None),
        P("dp", "seq", None),
        P("seq"),
        P("seq", None),
        P("seq", None),
        P("seq", None),
        P("seq", None),
        P("seq", None),
        P("seq", None),
        P("seq"),
        P("seq", None),
        P("seq"),
        P("seq", None),
        P("seq", None),
    )
    return jax.shard_map(body, mesh=mesh, in_specs=in_specs, out_specs=out_specs, check_vma=False)
```

profile of v0, /device:TPU:0, one launch (start us, length us, event | category | flops | bytes accessed | tf_op | source)
XLA Modules:
  0.0 1152.8 jit_solution(10320423289429418594)
XLA Ops:
  9.6 4.3 convolution_convert_fusion.12
  29.9 3.4 convolution_convert_fusion.10
  36.7 3.4 fusion.138
  44.2 3.7 collective-permute-start
  48.2 4.0 convolution_convert_fusion.8
  65.4 78.4 %all-gather.9.cloned.1.call-done = f32[4096,1024]{1,0:T(8,128)} async-done(((f32[512,1024]{1,0:T(8,128)}), f32[4096,1024]{1,0:T(8,128)}) %all-gather.9.cloned.1.call-update) | async-done | bytes 16777232 | tf_op jit(solution)/shard_map/all_gather | solution.py:26
  143.9 92.9 %all-gather.11.cloned.1.call-done = f32[4096,1024]{1,0:T(8,128)} async-done(((f32[512,1024]{1,0:T(8,128)}), f32[4096,1024]{1,0:T(8,128)}) %all-gather.11.cloned.1.call-update) | async-done | bytes 16777232 | tf_op jit(solution)/shard_map/all_gather | solution.py:26
  236.7 36.1 %while.29 = (s32[]{:T(128)}, f32[512,1024]{1,0:T(8,128)}, s32[]{:T(128)}, f32[8,512,1024]{2,1,0:T(8,128)}, f32[8,512,1024]{2,1,0:T(8,128)}, /*index=5*/s32[]{:T(128)}, s32[]{:T(128)}) while((s32[]{:T(128)}, f32[512,1024]{1,0:T(8,128)}, s32[]{:T(128)}, f32[8,512,1024]{2,1,0:T(8,128)}, f32[8,512,1024]{2,1,0:T(8,128)}, ...), condition=%wide.region_4.5_spmd.clone, body=%wide.region_3.4_spmd.clone.sunk | while | flops 2097156 | bytes 8388717 | solution.py:35
  236.7 4.5 fusion.206
  241.2 5.1 fusion.206
  246.3 5.5 fusion.206
  251.9 5.1 fusion.206
  257.0 5.1 fusion.206
  262.1 5.2 fusion.206
  267.3 5.6 fusion.206
  272.9 6.1 add_bitcast_fusion
  290.7 13.2 %fusion.142 = (f32[8,512]{1,0:T(8,128)S(1)}, f32[8,512,1536]{2,1,0:T(8,128)}) fusion(bf16[512,8,128]{0,2,1:T(8,128)(2,1)S(1)} %bitcast.282, bf16[1536,8,128]{2,0,1:T(8,128)(2,1)} %bitcast_dynamic-update-slice_fusion, pred[512,1536]{1,0:T(8,128)(4,1)S(1)} %copy-done.22), kind=kOutput, calls=%fused_computation.188 | convolution fusion | flops 1629483008 | bytes 30162944 | tf_op jit(solution)/shard_map/whd,khd->hwk/dot_general | solution.py:184
  303.9 11.4 fusion.6
  315.4 12.0 %fusion.96 = bf16[8,128,512]{2,1,0:T(8,128)(2,1)} fusion(f32[8,512,1536]{2,1,0:T(8,128)} %get-tuple-element.274, f32[8,512]{1,0:T(8,128)S(1)} %fusion.6, f32[8,512]{1,0:T(8,128)S(1)} %get-tuple-element.273, bf16[512,8,128]{0,2,1:T(8,128)(2,1)S(1)} %bitcast.299, bf16[512,8,128]{0,2,1:T(8,128)(2,1)S(1)} %bitcast.274, bf16[512,8,128]{0,2,1:T(8,128)(2,1)S(1)} %bitcast.297), kind=kOutput, calls=%fused_computation.134 | convolution fusion | flops 1639448576 | bytes 29392896 | tf_op jit(solution)/shard_map/hwk,khd->whd/dot_general | solution.py:191
  327.4 3.3 multiply_reduce_fusion.4
  330.7 11.1 fusion.130
  341.8 12.0 %fusion.19 = bf16[512,4096]{1,0:T(8,128)(2,1)S(1)} fusion(f32[512,4096]{1,0:T(8,128)} %fusion.130, bf16[4096,1024]{1,0:T(8,128)(2,1)} %param.33, bf16[1,512,1024]{2,1,0:T(8,128)(2,1)S(1)} %copy-done.36), kind=kOutput, calls=%fused_computation.28 | convolution fusion | flops 4339007488 | bytes 22020096 | tf_op jit(solution)/shard_map/dot_general | solution.py:85
  353.8 9.6 multiply_reduce_fusion.2
  370.0 16.5 %fusion.146 = (bf16[1536,8,128]{0,2,1:T(8,128)(2,1)}, f32[1536,8,128]{0,2,1:T(8,128)}) fusion(bf16[512,8,128]{0,2,1:T(8,128)(2,1)} %bitcast.276, f32[8,512,1536]{2,1,0:T(8,128)} %get-tuple-element.274, f32[8,512]{1,0:T(8,128)S(1)} %log_add_fusion.1), kind=kOutput, calls=%fused_computation.190 | convolution fusion | flops 1624768512 | bytes 35667968 | tf_op jit(solution)/shard_map/hwk,whd->khd/dot_general | solution.py:218
  389.7 10.1 fusion.99
  399.8 50.7 %fusion.143 = (bf16[1536,8,128]{0,2,1:T(8,128)(2,1)}, f32[1536,8,128]{0,2,1:T(8,128)}) fusion(bf16[512,8,128]{0,2,1:T(8,128)(2,1)} %bitcast.281, f32[8,512,1536]{2,1,0:T(8,128)} %fusion.99, f32[8,512,1536]{2,1,0:T(8,128)} %get-tuple-element.274, f32[8,512]{1,0:T(8,128)S(1)} %log_add_fusion.1), kind=kOutput, calls=%fused_computation.189 | convolution fusion | flops 1656231424 | bytes 60833792 | tf_op jit(solution)/shard_map/hwk,whd->khd/dot_general | solution.py:228
  457.0 3.2 fusion.87
  460.3 4.5 convolution_convert_fusion.4
  464.9 52.2 %fusion.93 = bf16[8,128,512]{2,1,0:T(8,128)(2,1)} fusion(bf16[1536,8,128]{2,0,1:T(8,128)(2,1)} %bitcast_dynamic-update-slice_fusion, f32[8,512,1536]{2,1,0:T(8,128)} %fusion.99, f32[8,512,1536]{2,1,0:T(8,128)} %get-tuple-element.274, f32[8,512]{1,0:T(8,128)S(1)} %log_add_fusion.1), kind=kOutput, calls=%fused_computation.132 | convolution fusion | flops 1655182848 | bytes 54542336 | tf_op jit(solution)/shard_map/hwk,khd->whd/dot_general | solution.py:224
  517.2 4.1 convolution_convert_fusion.5
  521.3 11.0 convolution_convert_fusion
  532.3 10.7 convolution_convert_fusion.1
  547.5 5.1 collective-permute-done.1
  552.6 4.3 convert_element_type.315
  558.5 29.0 %while.28 = (s32[]{:T(128)}, f32[512,1024]{1,0:T(8,128)}, s32[]{:T(128)}, bf16[8,512,1024]{2,1,0:T(8,128)(2,1)}, bf16[8,512,1024]{2,1,0:T(8,128)(2,1)}, /*index=5*/s32[]{:T(128)}, s32[]{:T(128)}, s32[]{:T(128)}, s32[]{:T(128)}) while((s32[]{:T(128)}, f32[512,1024]{1,0:T(8,128)}, s32[]{:T(128)}, bf16[8,512,1024]{2,1,0:T(8,128)(2,1)}, ...), condition=%wide.region_11.12_spmd, body=%wide.region_10.11_spmd.sunk | while | flops 2097158 | bytes 6291607 | solution.py:58
  558.5 4.1 convert_add_fusion.3
  562.6 4.1 convert_add_fusion.3
  566.7 4.1 convert_add_fusion.3
  570.8 4.3 convert_add_fusion.3
  575.1 4.3 convert_add_fusion.3
  579.4 4.1 convert_add_fusion.3
  583.4 4.1 convert_add_fusion.3
  587.5 7.9 fusion.137
  595.7 6.2 convolution_convert_fusion.13
  604.1 6.2 fusion.150
  610.3 17.7 %fusion.90 = bf16[8,128,512]{2,1,0:T(8,128)(2,1)} fusion(f32[8,512,512]{1,2,0:T(8,128)} %fusion.150, f32[8,512,512]{2,1,0:T(8,128)} %copy-done.1, f32[8,512]{1,0:T(8,128)S(1)} %log_add_fusion, bf16[512,1024]{1,0:T(8,128)(2,1)} %convolution_convert_fusion.12), kind=kOutput, calls=%fused_computation.131 | convolution fusion | flops 556274176 | bytes 18890752 | tf_op jit(solution)/shard_map/hnw,whd->nhd/dot_general | solution.py:260
  630.3 6.0 slice_add_fusion
  636.6 16.0 %slice_add_fusion.1 = f32[512,8,128]{0,2,1:T(8,128)} fusion(f32[1536,8,128]{0,2,1:T(8,128)} %get-tuple-element.279, bf16[512,8,128]{0,2,1:T(8,128)(2,1)} %bitcast.288, f32[8,512,512]{1,2,0:T(8,128)} %fusion.150, f32[8,512,512]{2,1,0:T(8,128)} %copy-done.1, f32[8,512]{1,0:T(8,128)S(1)} %log_add_fusion), kind=kOutput, calls=%fused_computation.85 | convolution fusion | flops 556274176 | bytes 38830080 | tf_op jit(solution)/shard_map/hnw,nhd->whd/dot_general | solution.py:263
  652.5 5.3 fusion.81
  667.8 6.2 convolution_convert_fusion.3
  674.4 6.5 reduce-scatter.26.cloned.1.call-done
  680.9 75.1 %reduce-scatter.24.cloned.1.call-done = bf16[128,4096]{1,0:T(8,128)(2,1)} async-done(((bf16[1024,4096]{1,0:T(8,128)(2,1)}), bf16[128,4096]{1,0:T(8,128)(2,1)}) %reduce-scatter.24.cloned.1.call-update) | async-done | bytes 1048592 | tf_op jit(solution)/shard_map/reduce_scatter | solution.py:317
  756.0 39.8 %reduce-scatter.22.cloned.1.call-done = bf16[64,1024]{1,0:T(8,128)(2,1)} async-done(((bf16[512,1024]{1,0:T(8,128)(2,1)}), bf16[64,1024]{1,0:T(8,128)(2,1)}) %reduce-scatter.22.cloned.1.call-update) | async-done | bytes 131088 | tf_op jit(solution)/shard_map/reduce_scatter | solution.py:311
  795.9 39.1 %reduce-scatter.18.cloned.1.call-done = bf16[64,1024]{1,0:T(8,128)(2,1)} async-done(((bf16[512,1024]{1,0:T(8,128)(2,1)}), bf16[64,1024]{1,0:T(8,128)(2,1)}) %reduce-scatter.18.cloned.1.call-update) | async-done | bytes 131088 | tf_op jit(solution)/shard_map/reduce_scatter | solution.py:302
  835.0 44.5 %reduce-scatter.14.cloned.1.call-done = bf16[128,1024]{1,0:T(8,128)(2,1)} async-done(((bf16[1024,1024]{1,0:T(8,128)(2,1)}), bf16[128,1024]{1,0:T(8,128)(2,1)}) %reduce-scatter.14.cloned.1.call-update) | async-done | bytes 262160 | tf_op jit(solution)/shard_map/reduce_scatter | solution.py:296
  879.5 44.7 %reduce-scatter.12.cloned.1.call-done = bf16[128,1024]{1,0:T(8,128)(2,1)} async-done(((bf16[1024,1024]{1,0:T(8,128)(2,1)}), bf16[128,1024]{1,0:T(8,128)(2,1)}) %reduce-scatter.12.cloned.1.call-update) | async-done | bytes 262160 | tf_op jit(solution)/shard_map/reduce_scatter | solution.py:293
  924.2 54.7 %reduce-scatter.20.cloned.1.call-done = bf16[128,2048]{1,0:T(8,128)(2,1)} async-done(((bf16[1024,2048]{1,0:T(8,128)(2,1)}), bf16[128,2048]{1,0:T(8,128)(2,1)}) %reduce-scatter.20.cloned.1.call-update) | async-done | bytes 524304 | tf_op jit(solution)/shard_map/reduce_scatter | solution.py:305
  980.2 3.4 fusion.148
  983.6 12.7 %fusion.98 = bf16[1,512,1024]{2,1,0:T(8,128)(2,1)} fusion(f32[512,1024]{1,0:T(8,128)S(1)} %copy-done.18, bf16[4096,1024]{1,0:T(8,128)(2,1)} %param.33, f32[512,4096]{1,0:T(8,128)} %fusion.130), kind=kOutput, calls=%fused_computation.136 | convolution fusion | flops 4314890240 | bytes 19922944 | tf_op jit(solution)/shard_map/dot_general | solution.py:75
  999.3 3.2 fusion.74
  1002.5 13.1 %all-reduce.3 = (bf16[1024]{0:T(1024)(128)(2,1)S(1)}, bf16[1024]{0:T(1024)(128)(2,1)S(1)}, bf16[1024]{0:T(1024)(128)(2,1)S(1)}) all-reduce(bf16[1024]{0:T(1024)(128)(2,1)S(1)} %get-tuple-element.215, bf16[1024]{0:T(1024)(128)(2,1)S(1)} %get-tuple-element.252, ...), channel_id=6, replica_groups=mesh['seq'=8,'dp'=4] {'seq'}, use_global_device_ids=true, to_apply=%region_15.16.clone | all-reduce | flops 3072 | bytes 12288
  1015.8 12.4 %all-reduce.4 = (bf16[128]{0:T(256)(128)(2,1)S(1)}, bf16[128]{0:T(256)(128)(2,1)S(1)}, bf16[128]{0:T(256)(128)(2,1)S(1)}) all-reduce(bf16[128]{0:T(256)(128)(2,1)S(1)} %dynamic-slice.1, bf16[128]{0:T(256)(128)(2,1)S(1)} %dynamic-slice.3, bf16[128]{0:T(256)(128)(2,1)S(1)} %dynamic-slice.5), channel_id=1, replica_groups=mesh['seq'=8,'dp'=4] {'dp'}, use_global_device_ids=true, to_apply=%region_16.17 | all-reduce | flops 384 | bytes 1536 | tf_op jit(solution)/shard_map/psum | solution.py:326
  1029.8 4.3 fusion.70
  1034.1 97.9 %all-reduce.8.cloned.1.call-done = (bf16[128,1024]{1,0:T(8,128)(2,1)}, bf16[128,1024]{1,0:T(8,128)(2,1)}, bf16[128,1024]{1,0:T(8,128)(2,1)}, bf16[128,1024]{1,0:...) async-done(((bf16[128,1024]{1,0:T(8,128)(2,1)}, ...) | async-done | bytes 3932176 | tf_op jit(solution)/shard_map/psum | solution.py:327
  (207 shorter events, 107.2 us)
Async XLA Ops:
  7.2 6.7 copy-start
  7.2 136.7 %all-gather.9.cloned.1.call-start = ((), (), s32[]{:S(2)}) async-start(), calls=%async_computation.18 | async-start | bytes 18874368 | tf_op jit(solution)/shard_map/all_gather | solution.py:26
  9.5 38.6 %copy-start.44 = (f32[512]{0:T(512)}, f32[512]{0:T(512)S(1)}, u32[]{:S(2)}) copy-start(f32[512]{0:T(512)S(1)} %add_rsqrt_fusion.1) | copy-start | bytes 6148
  9.6 4.3 copy-start.7
  9.6 4.3 copy-start.46
  23.5 3.3 copy-start.1
  23.5 3.4 copy-start.38
  26.9 3.0 copy-start.41
  29.9 4.4 copy-start.11
  34.3 2.4 copy-start.19
  34.3 2.4 copy-start.43
  36.7 3.6 copy-start.2
  40.3 196.4 %all-gather.11.cloned.1.call-start = ((), (), s32[]{:S(2)}) async-start(), calls=%async_computation.19 | async-start | bytes 18874368 | tf_op jit(solution)/shard_map/all_gather | solution.py:26
  41.1 515.8 %all-gather.13.cloned.1.call-start = ((), (), s32[]{:S(2)}) async-start(), calls=%async_computation.20 | async-start | bytes 9437184 | tf_op jit(solution)/shard_map/all_gather | solution.py:43
  44.2 12.0 %collective-permute-start = (bf16[2,512,1024]{2,1,0:T(8,128)(2,1)}, bf16[2,512,1024]{2,1,0:T(8,128)(2,1)}, u32[]{:S(2)}, u32[]{:S(2)}) collective-permute-start(bf16[2,512,1024]{2,1,0:T(8,128)(2,1)} %pad_maximum_fusion.1), channel_id=1, source_target_pairs={{0,4},{4,8},{8,12},{12,16},{16,20},{20,24},{24,28},{1,5},{5,9},{9,... | collective-permute-start | bytes 6291464 | tf_op jit(solution)/shard_map/ppermute | solution.py:21
  47.9 509.0 %all-gather.15.cloned.1.call-start = ((), (), s32[]{:S(2)}) async-start(), calls=%async_computation.21 | async-start | bytes 9437184 | tf_op jit(solution)/shard_map/all_gather | solution.py:43
  61.5 2.7 copy-start.12
  279.0 4.6 copy-start.6
  279.0 2.3 copy-start.50
  281.4 2.2 copy-start.13
  288.1 2.6 copy-start.21
  288.1 2.6 copy-start.22
  303.9 11.5 copy-start.8
  303.9 11.5 copy-start.28
  303.9 11.5 copy-start.30
  327.4 3.3 copy-start.48
  330.6 32.7 %copy-start.17 = (f32[512,1024]{1,0:T(8,128)}, f32[512,1024]{1,0:T(8,128)S(1)}, u32[]{:S(2)}) copy-start(f32[512,1024]{1,0:T(8,128)S(1)} %get-tuple-element.276) | copy-start | bytes 6291460
  330.7 11.1 copy-start.36
  353.8 9.6 copy-start.54
  386.5 3.2 copy-start.9
  386.5 3.2 copy-start.10
  386.5 3.2 copy-start.29
  386.5 3.2 copy-start.31
  450.6 2.9 copy-start.51
  453.4 2.6 copy-start.3
  453.4 2.9 copy-start.26
  453.5 3.5 copy-start.32
  460.3 214.1 %reduce-scatter.16.cloned.1.call-start = ((), (), s32[]{:S(2)}) async-start(), calls=%async_computation.12 | async-start | bytes 2359296 | tf_op jit(solution)/shard_map/reduce_scatter | solution.py:299
  464.8 52.3 %copy-start.45 = (f32[512]{0:T(512)S(1)}, f32[512]{0:T(512)}, u32[]{:S(2)}) copy-start(f32[512]{0:T(512)} %copy-done.44) | copy-start | bytes 6148
  464.9 52.3 %copy-start.47 = (f32[1024]{0:T(1024)S(1)}, f32[1024]{0:T(1024)}, u32[]{:S(2)}) copy-start(f32[1024]{0:T(1024)} %param.22) | copy-start | bytes 12292
  464.9 209.5 %reduce-scatter.10.cloned.1.call-start = ((), (), s32[]{:S(2)}) async-start(), calls=%async_computation.9 | async-start | bytes 2359296 | tf_op jit(solution)/shard_map/reduce_scatter | solution.py:290
  521.2 159.6 %reduce-scatter.26.cloned.1.call-start = ((), (), s32[]{:S(2)}) async-start(), calls=%async_computation.17 | async-start | bytes 9437184 | tf_op jit(solution)/shard_map/reduce_scatter | solution.py:320
  532.3 223.8 %reduce-scatter.24.cloned.1.call-start = ((), (), s32[]{:S(2)}) async-start(), calls=%async_computation.16 | async-start | bytes 9437184 | tf_op jit(solution)/shard_map/reduce_scatter | solution.py:317
  543.1 4.4 copy-start.39
  543.1 4.4 copy-start.42
  543.1 252.8 %reduce-scatter.22.cloned.1.call-start = ((), (), s32[]{:S(2)}) async-start(), calls=%async_computation.15 | async-start | bytes 1179648 | tf_op jit(solution)/shard_map/reduce_scatter | solution.py:311
  546.2 6.4 collective-permute-start.1
  595.5 239.5 %reduce-scatter.18.cloned.1.call-start = ((), (), s32[]{:S(2)}) async-start(), calls=%async_computation.13 | async-start | bytes 1179648 | tf_op jit(solution)/shard_map/reduce_scatter | solution.py:302
  636.3 243.1 %reduce-scatter.14.cloned.1.call-start = ((), (), s32[]{:S(2)}) async-start(), calls=%async_computation.11 | async-start | bytes 2359296 | tf_op jit(solution)/shard_map/reduce_scatter | solution.py:296
  662.1 262.1 %reduce-scatter.12.cloned.1.call-start = ((), (), s32[]{:S(2)}) async-start(), calls=%async_computation.10 | async-start | bytes 2359296 | tf_op jit(solution)/shard_map/reduce_scatter | solution.py:293
  662.1 2.9 copy-start.15
  662.1 2.9 copy-start.25
  667.8 311.2 %reduce-scatter.20.cloned.1.call-start = ((), (), s32[]{:S(2)}) async-start(), calls=%async_computation.14 | async-start | bytes 4718592 | tf_op jit(solution)/shard_map/reduce_scatter | solution.py:305
  674.0 305.0 %copy-start.53 = (u32[32]{0:T(128)S(1)}, u32[32]{0:T(128)}, u32[]{:S(2)}) copy-start(u32[32]{0:T(128)} %constant.106) | copy-start | bytes 388
  674.0 457.9 %all-reduce.8.cloned.1.call-start = ((), (), s32[]{:S(2)}) async-start(), calls=%async_computation.22 | async-start | bytes 7864320 | tf_op jit(solution)/shard_map/psum | solution.py:327
  980.2 3.4 copy-start.18
  983.6 12.8 %copy-start.4 = (f32[2,512,1024]{1,2,0:T(8,128)S(1)}, f32[2,512,1024]{1,2,0:T(8,128)}, u32[]{:S(2)}) copy-start(f32[2,512,1024]{1,2,0:T(8,128)} %convert_element_type.315) | copy-start | bytes 12582916
  983.6 12.8 %copy-start.5 = (f32[512,8,128]{0,2,1:T(8,128)S(1)}, f32[512,8,128]{0,2,1:T(8,128)}, u32[]{:S(2)}) copy-start(f32[512,8,128]{0,2,1:T(8,128)} %slice_add_fusion) | copy-start | bytes 6291460
  983.6 12.7 %copy-start.16 = (f32[512,8,128]{0,2,1:T(8,128)S(1)}, f32[512,8,128]{0,2,1:T(8,128)}, u32[]{:S(2)}) copy-start(f32[512,8,128]{0,2,1:T(8,128)} %slice_add_fusion.1) | copy-start | bytes 6291460
  999.3 3.2 copy-start.49
  1131.9 8.9 copy-start.40
  1131.9 9.7 copy-start.37
  1131.9 10.8 copy-start.35
  1138.9 5.3 copy-start.34
  (7 other events, 10.3 us)
Sparse Core Ops, SparseCore 0:
  40.4 103.3 all-gather.8
  146.3 90.3 all-gather.10
  238.6 54.3 all-gather.12
  460.4 55.1 all-gather.14
  518.7 42.5 reduce-scatter.15
  564.8 41.2 reduce-scatter.9
  609.5 71.2 reduce-scatter.25
  684.7 71.2 reduce-scatter.23
  759.8 36.0 reduce-scatter.21
  798.9 36.0 reduce-scatter.17
  838.2 41.1 reduce-scatter.13
  883.0 41.2 reduce-scatter.11
  927.6 51.3 reduce-scatter.19
  982.2 149.6 all-reduce.7
where the time goes:
time: 1160 us; the launch traced here: 1150 us
  waiting for transfers between devices  580 us (50%)
  matrix products  340 us (29%)
  other arithmetic  139 us (12%)
  local copies, waits for them, and re-layouts  45.9 us (4%)
  blocking collectives  25.5 us (2%)
  between operations  16.4 us (1%)
    all_gather x2, waiting for transfers between devices, entering(): pieces = jax.tree.map(lambda part: lax.all_gather(part, axis), value)  171 us
    psum x1, waiting for transfers between devices, body(): lax.psum(whole[1].astype(jnp.bfloat16), 'dp').astype(jnp.float32)  97.9 us
    reduce_scatter x1, waiting for transfers between devices, body(): lax.psum_scatter(up_grad.astype(jnp.bfloat16), 'seq', scatter_dimension=0...  75.1 us
    reduce_scatter x1, waiting for transfers between devices, body(): lax.psum_scatter(state_weight_grad.astype(jnp.bfloat16), 'seq', scatter_d...  54.7 us
    dot_general x1, matrix products, body(): jnp.einsum('hwk,khd->whd', score_grad, seen_keys, preferred_element_type=...  52.2 us
    dot_general x1, matrix products, body(): jnp.einsum('hwk,whd->khd', score_grad, token_heads, preferred_element_typ...  50.7 us
    dot_general x9, matrix products, product_tn(): lax.dot_general(left, right, (((0,), (0,)), ((), ())), preferred_element_...  46.2 us
    reduce_scatter x1, waiting for transfers between devices, body(): lax.psum_scatter(key_grad.astype(jnp.bfloat16), 'seq', scatter_dimension=...  44.7 us
  transfers between devices with their start and end apart: 16, of which 11 were waited for; matrix products, arithmetic and copies ran while one was open for 41% of the time, Pallas kernels for 0%

commit v1 on v0

--- a/solution.py
+++ b/solution.py
@@ -324,7 +324,9 @@
     summed = tuple(
         (
             lax.psum(whole[0].astype(jnp.bfloat16), "dp").astype(jnp.float32),
-            lax.psum(whole[1].astype(jnp.bfloat16), "dp").astype(jnp.float32),
+            jnp.sum(lax.all_gather(whole[1].astype(jnp.bfloat16), "dp"), axis=0).astype(
+                jnp.float32
+            ),
             lax.psum(whole[2].astype(jnp.bfloat16), "dp").astype(jnp.float32),
             lax.psum(whole[3].astype(jnp.bfloat16), "dp").astype(jnp.float32),
             lax.psum(whole[4].astype(jnp.bfloat16), "dp").astype(jnp.float32),

time: 1160 us -> 1180 us (1.017)
  waiting for transfers between devices: 580 us -> 594 us
    all_gather x0 -> x1, waiting for transfers between devices: none -> 12.7 us  [body(): lax.all_gather(whole[1].astype(jnp.bfloat16), 'dp')]
  transfers between devices with their start and end apart: 16 -> 17, of which waited for: 11 -> 12; matrix products, arithmetic and copies ran while one was open for 41% -> 41% of each run, Pallas kernels for 0% -> 0%
where the time goes in v1:
time: 1180 us; the launch traced here: 1170 us
  waiting for transfers between devices  594 us (50%)
  matrix products  340 us (29%)
  other arithmetic  143 us (12%)
  local copies, waits for them, and re-layouts  45.9 us (4%)
  blocking collectives  25.7 us (2%)
  between operations  16.4 us (1%)
    all_gather x2, waiting for transfers between devices, entering(): pieces = jax.tree.map(lambda part: lax.all_gather(part, axis), value)  171 us
    psum x1, waiting for transfers between devices, body(): lax.psum(whole[2].astype(jnp.bfloat16), 'dp').astype(jnp.float32)  100 us
    reduce_scatter x1, waiting for transfers between devices, body(): lax.psum_scatter(up_grad.astype(jnp.bfloat16), 'seq', scatter_dimension=0...  75.2 us
    reduce_scatter x1, waiting for transfers between devices, body(): lax.psum_scatter(state_weight_grad.astype(jnp.bfloat16), 'seq', scatter_d...  54.7 us
    dot_general x1, matrix products, body(): jnp.einsum('hwk,khd->whd', score_grad, seen_keys, preferred_element_type=...  52.3 us
    dot_general x1, matrix products, body(): jnp.einsum('hwk,whd->khd', score_grad, token_heads, preferred_element_typ...  50.8 us
    dot_general x9, matrix products, product_tn(): lax.dot_general(left, right, (((0,), (0,)), ((), ())), preferred_element_...  46.1 us
    reduce_scatter x1, waiting for transfers between devices, body(): lax.psum_scatter(key_grad.astype(jnp.bfloat16), 'seq', scatter_dimension=...  44.7 us
  transfers between devices with their start and end apart: 17, of which 12 were waited for; matrix products, arithmetic and copies ran while one was open for 41% of the time, Pallas kernels for 0%

profile of v1, /device:TPU:0, one launch (start us, length us, event | category | flops | bytes accessed | tf_op | source)
XLA Modules:
  0.0 1171.8 jit_solution(10904797699632642942)
XLA Ops:
  9.6 4.3 convolution_convert_fusion.12
  29.9 3.4 convolution_convert_fusion.10
  36.7 3.3 fusion.138
  44.1 3.7 collective-permute-start
  48.1 4.0 convolution_convert_fusion.8
  65.4 78.5 %all-gather.11.cloned.1.call-done = f32[4096,1024]{1,0:T(8,128)} async-done(((f32[512,1024]{1,0:T(8,128)}), f32[4096,1024]{1,0:T(8,128)}) %all-gather.11.cloned.1.call-update) | async-done | bytes 16777232 | tf_op jit(solution)/shard_map/all_gather | solution.py:26
  143.8 92.9 %all-gather.13.cloned.1.call-done = f32[4096,1024]{1,0:T(8,128)} async-done(((f32[512,1024]{1,0:T(8,128)}), f32[4096,1024]{1,0:T(8,128)}) %all-gather.13.cloned.1.call-update) | async-done | bytes 16777232 | tf_op jit(solution)/shard_map/all_gather | solution.py:26
  236.7 36.1 %while.29 = (s32[]{:T(128)}, f32[512,1024]{1,0:T(8,128)}, s32[]{:T(128)}, f32[8,512,1024]{2,1,0:T(8,128)}, f32[8,512,1024]{2,1,0:T(8,128)}, /*index=5*/s32[]{:T(128)}, s32[]{:T(128)}) while((s32[]{:T(128)}, f32[512,1024]{1,0:T(8,128)}, s32[]{:T(128)}, f32[8,512,1024]{2,1,0:T(8,128)}, f32[8,512,1024]{2,1,0:T(8,128)}, ...), condition=%wide.region_4.5_spmd.clone, body=%wide.region_3.4_spmd.clone.sunk | while | flops 2097156 | bytes 8388717 | solution.py:35
  236.7 4.5 fusion.206
  241.2 5.1 fusion.206
  246.3 5.5 fusion.206
  251.8 5.1 fusion.206
  256.9 5.1 fusion.206
  262.0 5.2 fusion.206
  267.2 5.6 fusion.206
  272.8 6.1 add_bitcast_fusion
  290.7 13.2 %fusion.142 = (f32[8,512]{1,0:T(8,128)S(1)}, f32[8,512,1536]{2,1,0:T(8,128)}) fusion(bf16[512,8,128]{0,2,1:T(8,128)(2,1)S(1)} %bitcast.283, bf16[1536,8,128]{2,0,1:T(8,128)(2,1)} %bitcast_dynamic-update-slice_fusion, pred[512,1536]{1,0:T(8,128)(4,1)S(1)} %copy-done.19), kind=kOutput, calls=%fused_computation.188 | convolution fusion | flops 1629483008 | bytes 30162944 | tf_op jit(solution)/shard_map/whd,khd->hwk/dot_general | solution.py:184
  303.9 11.4 fusion.6
  315.4 12.0 %fusion.96 = bf16[8,128,512]{2,1,0:T(8,128)(2,1)} fusion(f32[8,512,1536]{2,1,0:T(8,128)} %get-tuple-element.273, f32[8,512]{1,0:T(8,128)S(1)} %fusion.6, f32[8,512]{1,0:T(8,128)S(1)} %get-tuple-element.272, bf16[512,8,128]{0,2,1:T(8,128)(2,1)S(1)} %bitcast.300, bf16[512,8,128]{0,2,1:T(8,128)(2,1)S(1)} %bitcast.275, bf16[512,8,128]{0,2,1:T(8,128)(2,1)S(1)} %bitcast.298), kind=kOutput, calls=%fused_computation.134 | convolution fusion | flops 1639448576 | bytes 29392896 | tf_op jit(solution)/shard_map/hwk,khd->whd/dot_general | solution.py:191
  330.7 11.1 fusion.130
  341.7 12.0 %fusion.19 = bf16[512,4096]{1,0:T(8,128)(2,1)S(1)} fusion(f32[512,4096]{1,0:T(8,128)} %fusion.130, bf16[4096,1024]{1,0:T(8,128)(2,1)} %param.33, bf16[1,512,1024]{2,1,0:T(8,128)(2,1)S(1)} %copy-done.34), kind=kOutput, calls=%fused_computation.28 | convolution fusion | flops 4339007488 | bytes 22020096 | tf_op jit(solution)/shard_map/dot_general | solution.py:85
  353.8 9.6 multiply_reduce_fusion.2
  370.0 16.5 %fusion.146 = (bf16[1536,8,128]{0,2,1:T(8,128)(2,1)}, f32[1536,8,128]{0,2,1:T(8,128)}) fusion(bf16[512,8,128]{0,2,1:T(8,128)(2,1)} %bitcast.277, f32[8,512,1536]{2,1,0:T(8,128)} %get-tuple-element.273, f32[8,512]{1,0:T(8,128)S(1)} %log_add_fusion.1), kind=kOutput, calls=%fused_computation.190 | convolution fusion | flops 1624768512 | bytes 35667968 | tf_op jit(solution)/shard_map/hwk,whd->khd/dot_general | solution.py:218
  389.7 10.1 fusion.99
  399.8 50.8 %fusion.143 = (bf16[1536,8,128]{0,2,1:T(8,128)(2,1)}, f32[1536,8,128]{0,2,1:T(8,128)}) fusion(bf16[512,8,128]{0,2,1:T(8,128)(2,1)} %bitcast.282, f32[8,512,1536]{2,1,0:T(8,128)} %fusion.99, f32[8,512,1536]{2,1,0:T(8,128)} %get-tuple-element.273, f32[8,512]{1,0:T(8,128)S(1)} %log_add_fusion.1), kind=kOutput, calls=%fused_computation.189 | convolution fusion | flops 1656231424 | bytes 60833792 | tf_op jit(solution)/shard_map/hwk,whd->khd/dot_general | solution.py:228
  457.0 3.3 fusion.87
  460.4 52.3 %fusion.93 = bf16[8,128,512]{2,1,0:T(8,128)(2,1)} fusion(bf16[1536,8,128]{2,0,1:T(8,128)(2,1)} %bitcast_dynamic-update-slice_fusion, f32[8,512,1536]{2,1,0:T(8,128)} %fusion.99, f32[8,512,1536]{2,1,0:T(8,128)} %get-tuple-element.273, f32[8,512]{1,0:T(8,128)S(1)} %log_add_fusion.1), kind=kOutput, calls=%fused_computation.132 | convolution fusion | flops 1655182848 | bytes 54542336 | tf_op jit(solution)/shard_map/hwk,khd->whd/dot_general | solution.py:224
  512.7 4.0 convolution_convert_fusion.5
  516.8 4.5 convolution_convert_fusion.4
  521.3 10.9 convolution_convert_fusion
  532.4 10.7 convolution_convert_fusion.1
  547.5 5.1 collective-permute-done.1
  552.6 4.3 convert_element_type.317
  558.4 28.8 %while.28 = (s32[]{:T(128)}, f32[512,1024]{1,0:T(8,128)}, s32[]{:T(128)}, bf16[8,512,1024]{2,1,0:T(8,128)(2,1)}, bf16[8,512,1024]{2,1,0:T(8,128)(2,1)}, /*index=5*/s32[]{:T(128)}, s32[]{:T(128)}, s32[]{:T(128)}, s32[]{:T(128)}) while((s32[]{:T(128)}, f32[512,1024]{1,0:T(8,128)}, s32[]{:T(128)}, bf16[8,512,1024]{2,1,0:T(8,128)(2,1)}, ...), condition=%wide.region_11.12_spmd, body=%wide.region_10.11_spmd.sunk | while | flops 2097158 | bytes 6291607 | solution.py:58
  558.4 4.1 convert_add_fusion.3
  562.5 4.0 convert_add_fusion.3
  566.5 4.0 convert_add_fusion.3
  570.6 4.3 convert_add_fusion.3
  574.8 4.3 convert_add_fusion.3
  579.1 4.0 convert_add_fusion.3
  583.2 4.0 convert_add_fusion.3
  587.2 7.9 fusion.137
  595.4 6.2 convolution_convert_fusion.13
  603.8 6.1 fusion.150
  610.0 17.6 %fusion.90 = bf16[8,128,512]{2,1,0:T(8,128)(2,1)} fusion(f32[8,512,512]{1,2,0:T(8,128)} %fusion.150, f32[8,512,512]{2,1,0:T(8,128)} %copy-done.1, f32[8,512]{1,0:T(8,128)S(1)} %log_add_fusion, bf16[512,1024]{1,0:T(8,128)(2,1)} %convolution_convert_fusion.12), kind=kOutput, calls=%fused_computation.131 | convolution fusion | flops 556274176 | bytes 18890752 | tf_op jit(solution)/shard_map/hnw,whd->nhd/dot_general | solution.py:260
  629.9 6.0 slice_add_fusion
  636.2 15.9 %slice_add_fusion.1 = f32[512,8,128]{0,2,1:T(8,128)} fusion(f32[1536,8,128]{0,2,1:T(8,128)} %get-tuple-element.278, bf16[512,8,128]{0,2,1:T(8,128)(2,1)} %bitcast.289, f32[8,512,512]{1,2,0:T(8,128)} %fusion.150, f32[8,512,512]{2,1,0:T(8,128)} %copy-done.1, f32[8,512]{1,0:T(8,128)S(1)} %log_add_fusion), kind=kOutput, calls=%fused_computation.85 | convolution fusion | flops 556274176 | bytes 38830080 | tf_op jit(solution)/shard_map/hnw,nhd->whd/dot_general | solution.py:263
  652.1 5.2 fusion.81
  667.3 6.2 convolution_convert_fusion.3
  675.7 5.2 reduce-scatter.26.cloned.1.call-done
  680.9 75.2 %reduce-scatter.24.cloned.1.call-done = bf16[128,4096]{1,0:T(8,128)(2,1)} async-done(((bf16[1024,4096]{1,0:T(8,128)(2,1)}), bf16[128,4096]{1,0:T(8,128)(2,1)}) %reduce-scatter.24.cloned.1.call-update) | async-done | bytes 1048592 | tf_op jit(solution)/shard_map/reduce_scatter | solution.py:317
  756.1 39.8 %reduce-scatter.22.cloned.1.call-done = bf16[64,1024]{1,0:T(8,128)(2,1)} async-done(((bf16[512,1024]{1,0:T(8,128)(2,1)}), bf16[64,1024]{1,0:T(8,128)(2,1)}) %reduce-scatter.22.cloned.1.call-update) | async-done | bytes 131088 | tf_op jit(solution)/shard_map/reduce_scatter | solution.py:311
  795.9 39.1 %reduce-scatter.18.cloned.1.call-done = bf16[64,1024]{1,0:T(8,128)(2,1)} async-done(((bf16[512,1024]{1,0:T(8,128)(2,1)}), bf16[64,1024]{1,0:T(8,128)(2,1)}) %reduce-scatter.18.cloned.1.call-update) | async-done | bytes 131088 | tf_op jit(solution)/shard_map/reduce_scatter | solution.py:302
  835.0 44.5 %reduce-scatter.14.cloned.1.call-done = bf16[128,1024]{1,0:T(8,128)(2,1)} async-done(((bf16[1024,1024]{1,0:T(8,128)(2,1)}), bf16[128,1024]{1,0:T(8,128)(2,1)}) %reduce-scatter.14.cloned.1.call-update) | async-done | bytes 262160 | tf_op jit(solution)/shard_map/reduce_scatter | solution.py:296
  879.5 44.7 %reduce-scatter.12.cloned.1.call-done = bf16[128,1024]{1,0:T(8,128)(2,1)} async-done(((bf16[1024,1024]{1,0:T(8,128)(2,1)}), bf16[128,1024]{1,0:T(8,128)(2,1)}) %reduce-scatter.12.cloned.1.call-update) | async-done | bytes 262160 | tf_op jit(solution)/shard_map/reduce_scatter | solution.py:293
  924.2 54.7 %reduce-scatter.20.cloned.1.call-done = bf16[128,2048]{1,0:T(8,128)(2,1)} async-done(((bf16[1024,2048]{1,0:T(8,128)(2,1)}), bf16[128,2048]{1,0:T(8,128)(2,1)}) %reduce-scatter.20.cloned.1.call-update) | async-done | bytes 524304 | tf_op jit(solution)/shard_map/reduce_scatter | solution.py:305
  979.0 4.7 fusion.148
  983.6 12.1 %fusion.98 = bf16[1,512,1024]{2,1,0:T(8,128)(2,1)} fusion(f32[512,1024]{1,0:T(8,128)S(1)} %copy-done.15, bf16[4096,1024]{1,0:T(8,128)(2,1)} %param.33, f32[512,4096]{1,0:T(8,128)} %fusion.130), kind=kOutput, calls=%fused_computation.136 | convolution fusion | flops 4314890240 | bytes 19922944 | tf_op jit(solution)/shard_map/dot_general | solution.py:75
  995.8 12.7 %all-gather.19.cloned.1.call-done = bf16[512,1024]{1,0:T(8,128)(2,1)} async-done(((bf16[128,1024]{1,0:T(8,128)(2,1)}), bf16[512,1024]{1,0:T(8,128)(2,1)}) %all-gather.19.cloned.1.call-update) | async-done | bytes 1048592 | tf_op jit(solution)/shard_map/all_gather | solution.py:327
  1010.7 4.3 fusion.83
  1019.9 14.4 %all-reduce.3 = (bf16[1024]{0:T(1024)(128)(2,1)S(1)}, bf16[1024]{0:T(1024)(128)(2,1)S(1)}, bf16[1024]{0:T(1024)(128)(2,1)S(1)}) all-reduce(bf16[1024]{0:T(1024)(128)(2,1)S(1)} %get-tuple-element.215, bf16[1024]{0:T(1024)(128)(2,1)S(1)} %get-tuple-element.251, ...), channel_id=7, replica_groups=mesh['seq'=8,'dp'=4] {'seq'}, use_global_device_ids=true, to_apply=%region_15.16.clone | all-reduce | flops 3072 | bytes 12288
  1034.6 11.3 all-reduce.4
  1047.4 4.2 fusion.70
  1051.6 100.2 %all-reduce.8.cloned.1.call-done = (bf16[128,1024]{1,0:T(8,128)(2,1)}, bf16[128,1024]{1,0:T(8,128)(2,1)}, bf16[128,1024]{1,0:T(8,128)(2,1)}, bf16[64,1024]{1,0:T...) async-done(((bf16[128,1024]{1,0:T(8,128)(2,1)}, bf16[128,1024]{1,0:T(8,128)(2,1)}, ...) | async-done | bytes 3670032 | tf_op jit(solution)/shard_map/psum | solution.py:330
  (205 shorter events, 114.4 us)
Async XLA Ops:
  7.2 6.7 copy-start
  7.2 136.6 %all-gather.11.cloned.1.call-start = ((), (), s32[]{:S(2)}) async-start(), calls=%async_computation.18 | async-start | bytes 18874368 | tf_op jit(solution)/shard_map/all_gather | solution.py:26
  9.5 38.6 %copy-start.41 = (f32[512]{0:T(512)}, f32[512]{0:T(512)S(1)}, u32[]{:S(2)}) copy-start(f32[512]{0:T(512)S(1)} %add_rsqrt_fusion.1) | copy-start | bytes 6148
  9.6 4.3 copy-start.5
  9.6 4.3 copy-start.43
  23.5 3.2 copy-start.1
  23.5 3.4 copy-start.36
  26.9 3.0 copy-start.38
  29.9 4.4 copy-start.9
  34.3 2.4 copy-start.16
  34.3 2.4 copy-start.40
  36.7 3.6 copy-start.2
  40.3 196.4 %all-gather.13.cloned.1.call-start = ((), (), s32[]{:S(2)}) async-start(), calls=%async_computation.19 | async-start | bytes 18874368 | tf_op jit(solution)/shard_map/all_gather | solution.py:26
  41.0 515.8 %all-gather.15.cloned.1.call-start = ((), (), s32[]{:S(2)}) async-start(), calls=%async_computation.20 | async-start | bytes 9437184 | tf_op jit(solution)/shard_map/all_gather | solution.py:43
  44.1 12.0 %collective-permute-start = (bf16[2,512,1024]{2,1,0:T(8,128)(2,1)}, bf16[2,512,1024]{2,1,0:T(8,128)(2,1)}, u32[]{:S(2)}, u32[]{:S(2)}) collective-permute-start(bf16[2,512,1024]{2,1,0:T(8,128)(2,1)} %pad_maximum_fusion.1), channel_id=1, source_target_pairs={{0,4},{4,8},{8,12},{12,16},{16,20},{20,24},{24,28},{1,5},{5,9},{9,... | collective-permute-start | bytes 6291464 | tf_op jit(solution)/shard_map/ppermute | solution.py:21
  47.8 509.0 %all-gather.17.cloned.1.call-start = ((), (), s32[]{:S(2)}) async-start(), calls=%async_computation.21 | async-start | bytes 9437184 | tf_op jit(solution)/shard_map/all_gather | solution.py:43
  61.5 2.7 copy-start.10
  279.0 4.6 copy-start.4
  279.0 2.3 copy-start.47
  281.3 2.2 copy-start.11
  288.1 2.6 copy-start.18
  288.1 2.6 copy-start.19
  303.9 11.5 copy-start.6
  303.9 11.5 copy-start.25
  303.9 11.5 copy-start.27
  327.3 3.3 copy-start.45
  330.6 32.7 %copy-start.14 = (f32[512,1024]{1,0:T(8,128)}, f32[512,1024]{1,0:T(8,128)S(1)}, u32[]{:S(2)}) copy-start(f32[512,1024]{1,0:T(8,128)S(1)} %get-tuple-element.275) | copy-start | bytes 6291460
  330.7 11.1 copy-start.34
  353.7 9.6 copy-start.51
  363.3 2.0 copy-start.31
  386.5 3.2 copy-start.7
  386.5 3.2 copy-start.8
  386.5 3.2 copy-start.26
  386.5 3.2 copy-start.28
  450.6 2.9 copy-start.48
  453.5 2.6 copy-start.3
  453.5 2.9 copy-start.23
  453.5 3.5 copy-start.29
  460.3 52.4 %copy-start.42 = (f32[512]{0:T(512)S(1)}, f32[512]{0:T(512)}, u32[]{:S(2)}) copy-start(f32[512]{0:T(512)} %copy-done.41) | copy-start | bytes 6148
  460.3 52.4 %copy-start.44 = (f32[1024]{0:T(1024)S(1)}, f32[1024]{0:T(1024)}, u32[]{:S(2)}) copy-start(f32[1024]{0:T(1024)} %param.22) | copy-start | bytes 12292
  460.3 213.3 %reduce-scatter.10.cloned.1.call-start = ((), (), s32[]{:S(2)}) async-start(), calls=%async_computation.9 | async-start | bytes 2359296 | tf_op jit(solution)/shard_map/reduce_scatter | solution.py:290
  516.7 159.0 %reduce-scatter.16.cloned.1.call-start = ((), (), s32[]{:S(2)}) async-start(), calls=%async_computation.12 | async-start | bytes 2359296 | tf_op jit(solution)/shard_map/reduce_scatter | solution.py:299
  521.3 159.6 %reduce-scatter.26.cloned.1.call-start = ((), (), s32[]{:S(2)}) async-start(), calls=%async_computation.17 | async-start | bytes 9437184 | tf_op jit(solution)/shard_map/reduce_scatter | solution.py:320
  532.3 223.8 %reduce-scatter.24.cloned.1.call-start = ((), (), s32[]{:S(2)}) async-start(), calls=%async_computation.16 | async-start | bytes 9437184 | tf_op jit(solution)/shard_map/reduce_scatter | solution.py:317
  543.1 4.4 copy-start.37
  543.1 4.4 copy-start.39
  543.1 252.7 %reduce-scatter.22.cloned.1.call-start = ((), (), s32[]{:S(2)}) async-start(), calls=%async_computation.15 | async-start | bytes 1179648 | tf_op jit(solution)/shard_map/reduce_scatter | solution.py:311
  546.2 6.4 collective-permute-start.1
  595.1 239.8 %reduce-scatter.18.cloned.1.call-start = ((), (), s32[]{:S(2)}) async-start(), calls=%async_computation.13 | async-start | bytes 1179648 | tf_op jit(solution)/shard_map/reduce_scatter | solution.py:302
  635.9 243.6 %reduce-scatter.14.cloned.1.call-start = ((), (), s32[]{:S(2)}) async-start(), calls=%async_computation.11 | async-start | bytes 2359296 | tf_op jit(solution)/shard_map/reduce_scatter | solution.py:296
  657.3 1.6 copy-start.24
  661.6 262.6 %reduce-scatter.12.cloned.1.call-start = ((), (), s32[]{:S(2)}) async-start(), calls=%async_computation.10 | async-start | bytes 2359296 | tf_op jit(solution)/shard_map/reduce_scatter | solution.py:293
  661.7 2.9 copy-start.13
  661.7 2.9 copy-start.22
  667.3 311.6 %reduce-scatter.20.cloned.1.call-start = ((), (), s32[]{:S(2)}) async-start(), calls=%async_computation.14 | async-start | bytes 4718592 | tf_op jit(solution)/shard_map/reduce_scatter | solution.py:305
  673.5 334.9 %all-gather.19.cloned.1.call-start = ((), (), s32[]{:S(2)}) async-start(), calls=%async_computation.22 | async-start | bytes 1310720 | tf_op jit(solution)/shard_map/all_gather | solution.py:327
  674.1 477.7 %all-reduce.8.cloned.1.call-start = ((), (), s32[]{:S(2)}) async-start(), calls=%async_computation.23 | async-start | bytes 7340032 | tf_op jit(solution)/shard_map/psum | solution.py:330
  979.0 4.7 copy-start.15
  1010.7 4.3 copy-start.49
  1015.0 1.7 copy-start.30
  1016.7 3.2 copy-start.46
  1151.8 8.8 copy-start.35
  1151.8 9.9 copy-start.33
  1157.0 6.3 copy-start.32
  (5 other events, 6.0 us)
Sparse Core Ops, SparseCore 0:
  40.4 103.3 all-gather.10
  146.3 90.3 all-gather.12
  238.6 54.3 all-gather.14
  460.4 55.0 all-gather.16
  518.7 42.5 reduce-scatter.9
  564.8 41.2 reduce-scatter.15
  609.6 71.2 reduce-scatter.25
  684.8 71.2 reduce-scatter.23
  759.9 35.9 reduce-scatter.21
  798.9 36.0 reduce-scatter.17
  838.3 41.1 reduce-scatter.13
  883.0 41.2 reduce-scatter.11
  927.6 51.2 reduce-scatter.19
  980.4 27.9 all-gather.18
  1011.5 140.2 all-reduce.7
